TPU v7x, 256 devices: a whole 4x4x8 slice. The times are simulated.
256 devices in a mesh: smp: 32 (over x_lo, z, core), par: 8 (over x_hi, y).
Axes of the slice: x: 4 (x_hi: 2, x_lo: 2; x = x_hi * 2 + x_lo), y: 4, z: 8, core: 2. Of those that a mesh axis runs over, the one named last changes fastest.
Arguments:
- log_derivs: float32 [8192, 8192], P('smp', 'par'), may hold values from -40 to 40, as said below
- coefficients: float32 [8192], P('smp'), may hold values from -6 to 6
Outputs:
- gram: float32 [8192, 8192], P('smp', 'par')
- update: float32 [8192], P(('par', 'smp'))
Inputs may be any that keep to these rules, and one draw needn't show every extreme that they name: `log_derivs`: finite real values.
All inputs are finite; a program needn't handle non-finite values.
Results may differ from a plain program's by a relative error of at most 0.00014.
Values sent between devices are 32-bit elements; how exact they have to be, the bound alone decides.
A program may use at most 128 MiB of HBM per device.

v0:
```python
import jax
import jax.numpy as jnp
from jax import lax
from jax.sharding import PartitionSpec as P


def row_products(left_rows, right_rows):
    return lax.dot_general(
        left_rows,
        right_rows,
        (((1,), (1,)), ((), ())),
        precision=lax.Precision.HIGHEST,
        preferred_element_type=jnp.float32,
    )


def local(log_derivs, coefficients):
    samples = log_derivs.shape[0] * lax.axis_size("smp")
    column_total = lax.psum(jnp.sum(log_derivs, axis=0), "smp")
    centred = (log_derivs - column_total[None, :] / samples) / jnp.sqrt(jnp.float32(samples))
    partial_gram = row_products(centred, lax.all_gather(centred, "smp", axis=0, tiled=True))
    gram = lax.psum_scatter(partial_gram, "par", scatter_dimension=1, tiled=True)
    update_term = lax.dot_general(
        coefficients,
        centred,
        (((0,), (0,)), ((), ())),
        precision=lax.Precision.HIGHEST,
        preferred_element_type=jnp.float32,
    )
    update = lax.psum_scatter(update_term, "smp", scatter_dimension=0, tiled=True)
    return (gram, update)


def solution(mesh):
    placed = (P("smp", "par"), P("smp"))
    return jax.shard_map(
        local,
        mesh=mesh,
        in_specs=placed,
        out_specs=(P("smp", "par"), P(("par", "smp"))),
        check_vma=False,
    )
```

profile of v0, /device:TPU:8, one launch (start us, length us, event | category | flops | bytes accessed | tf_op | source)
XLA Modules:
  0.0 409.3 jit_solution(7156183414748305137)
XLA Ops:
  7.2 0.0 copy-start
  7.2 0.0 all-gather.2.cloned.1.call-start
  7.2 1.3 reduce_sum.9
  8.5 59.2 %psum.7 = f32[1024]{0:T(1024)S(1)} all-reduce(f32[1024]{0:T(1024)S(1)} %reduce_sum.9), channel_id=1, replica_groups=mesh['smp'=32,'par'=8] {'smp'}, use_global_device_ids=true, to_apply=%region_1.0 | all-reduce | flops 1024 | bytes 8192 | tf_op jit(solution)/shard_map/psum | solution.py:19
  67.7 2.4 subtract_multiply_fusion
  70.1 0.0 all-gather.2.cloned.1.call-update
  70.1 0.0 copy-start.2
  70.2 0.0 copy-start.1
  70.2 0.0 reduce-scatter.2.cloned.1.call-start
  70.2 180.2 %all-gather.2.cloned.1.call-done = f32[8192,1024]{1,0:T(8,128)} async-done(((f32[256,1024]{1,0:T(8,128)}), f32[8192,1024]{1,0:T(8,128)}) %all-gather.2.cloned.1.call-update) | async-done | bytes 33554448 | tf_op jit(solution)/shard_map/all_gather | solution.py:21
  250.4 33.2 %fusion = f32[256,8192]{1,0:T(8,128)} fusion(f32[256,1024]{1,0:T(8,128)} %subtract_multiply_fusion, f32[8192,1024]{1,0:T(8,128)} %all-gather.2.cloned.1.call-done), kind=kOutput, calls=%fused_computation.2 | convolution fusion | flops 25769803776 | bytes 42991616 | tf_op jit(solution)/shard_map/dot_general | solution.py:8
  283.6 0.0 reduce-scatter.2.cloned.1.call-update
  283.6 0.0 copy-done.2
  283.7 0.6 dynamic-slice
  284.9 0.0 copy-done
  284.9 0.0 copy-done.1
  284.9 0.6 fusion.1
  285.6 57.8 %all-reduce = f32[1024]{0:T(1024)S(1)} all-reduce(f32[1024]{0:T(1024)S(1)} %bitcast.8), channel_id=3, replica_groups=mesh['smp'=32,'par'=8] {'smp'}, use_global_device_ids=true, to_apply=%region_3.0.clone | all-reduce | flops 1024 | bytes 8192
  343.3 0.6 dynamic-slice.1
  343.9 58.5 %reduce-scatter.2.cloned.1.call-done = f32[256,1024]{1,0:T(8,128)} async-done(((f32[256,8192]{1,0:T(8,128)}), f32[256,1024]{1,0:T(8,128)}) %reduce-scatter.2.cloned.1.call-update) | async-done | bytes 1048592 | tf_op jit(solution)/shard_map/reduce_scatter | solution.py:22
  (1 shorter events, 0.0 us)
Async XLA Ops:
  7.2 277.7 %copy-start = (f32[256]{0:T(256)S(1)}, f32[256]{0:T(256)}, u32[]{:S(2)}) copy-start(f32[256]{0:T(256)} %param.3) | copy-start | bytes 3076
  7.2 243.2 %all-gather.2.cloned.1.call-start = ((), (), s32[]{:S(2)}) async-start(), calls=%async_computation.1 | async-start | bytes 34603008 | tf_op jit(solution)/shard_map/all_gather | solution.py:21
  70.1 213.5 %copy-start.2 = (u32[256]{0:T(256)S(1)}, u32[256]{0:T(256)}, u32[]{:S(2)}) copy-start(u32[256]{0:T(256)} %constant.10) | copy-start | bytes 3076
  70.2 214.7 %copy-start.1 = (f32[256,1024]{1,0:T(8,128)S(1)}, f32[256,1024]{1,0:T(8,128)}, u32[]{:S(2)}) copy-start(f32[256,1024]{1,0:T(8,128)} %subtract_multiply_fusion) | copy-start | bytes 3145732
  70.2 332.3 %reduce-scatter.2.cloned.1.call-start = ((), (), s32[]{:S(2)}) async-start(), calls=%async_computation.2 | async-start | bytes 9437184 | tf_op jit(solution)/shard_map/reduce_scatter | solution.py:22
Sparse Core Ops, SparseCore 0:
  70.3 180.0 all-gather.1
  283.8 118.6 reduce-scatter.1
where the time goes:
time: 411 us; the launch traced here: 409 us
  waiting for transfers between devices  239 us (58%)
  blocking collectives  117 us (28%)
  matrix products  33.9 us (8%)
  between operations  14.7 us (4%)
    all_gather x1, waiting for transfers between devices, local(): lax.all_gather(centred, 'smp', axis=0, tiled=True)  180 us
    psum x1, blocking collectives, local(): column_total = lax.psum(jnp.sum(log_derivs, axis=0), 'smp')  59.2 us
    reduce_scatter x1, waiting for transfers between devices, local(): lax.psum_scatter(partial_gram, 'par', scatter_dimension=1, tiled=True)  58.5 us
    unnamed x1, blocking collectives  57.8 us
    dot_general x1, matrix products, row_products(): lax.dot_general(left_rows, right_rows, (((1,), (1,)), ((), ())), precisio...  33.2 us
  transfers between devices with their start and end apart: 2, of which 2 were waited for; matrix products, arithmetic and copies ran while one was open for 0% of the time, Pallas kernels for 0%

commit v1 on v0

v1 whole, which is shorter than its diff:
```python
import functools

import jax
import jax.numpy as jnp
from jax import lax
from jax.experimental import pallas as pl
from jax.experimental.pallas import tpu as pltpu
from jax.sharding import PartitionSpec as P

MESH = pl.DeviceIdType.MESH
NZ, NY = 8, 4
BLOCKS = 8
CHUNKS = 16
CHUNK_ROWS, LANES = 64, 128
STEPS = BLOCKS * CHUNKS
LAG = 4
LATE = 7 * LAG
COMPUTE_AT = CHUNKS + LATE + 8
COMPUTE_END = COMPUTE_AT + BLOCKS * CHUNKS


def merge(stats):
    count = stats.shape[0]
    mean = jnp.sum(stats[:, 0:1, :], axis=0) * (1.0 / count)
    shift = stats[:, 0:1, :] - mean[None]
    update = jnp.sum(stats[:, 1:2, :] + stats[:, 2:3, :] * shift, axis=0)
    weight = jnp.sum(stats[:, 2:3, :], axis=0)
    return mean, update, weight


def split(values):
    high = values.astype(jnp.bfloat16)
    low = (values - high.astype(jnp.float32)).astype(jnp.bfloat16)
    return high, low


def product(left, right):
    return lax.dot_general(left, right, (((1,), (1,)), ((), ())), preferred_element_type=jnp.float32)


def kernel(
    x_ref, coef_ref, gram_ref, update_ref,
    rows, cols, part, landed, row_hi, row_lo, col_hi, col_lo, near, ring, means,
    load_sem, near_send, near_recv, ring_send, ring_recv, mean_send, mean_recv,
    row_send, row_recv, half_send, half_recv, share_send,
    send, recv, extra_send, extra_recv, part_send, part_recv,
):
    smp, par = lax.axis_index("smp"), lax.axis_index("par")
    core, z, xl = lax.rem(smp, 2), lax.rem(smp // 2, NZ), smp // (2 * NZ)
    y, xh = lax.rem(par, NY), par // NY
    h = lax.rem(z - 2 * y + NZ, NZ)

    def at(dz=0, dy=0, dc=0, dxl=0, dxh=0):
        zz, yy = lax.rem(z + dz + NZ, NZ), lax.rem(y + dy + NY, NY)
        cc, ll, hh = lax.rem(core + dc, 2), lax.rem(xl + dxl, 2), lax.rem(xh + dxh, 2)
        return {"smp": (ll * NZ + zz) * 2 + cc, "par": hh * NY + yy}

    def remote(src, dst, s_sem, r_sem, device):
        return pltpu.make_async_remote_copy(
            src_ref=src, dst_ref=dst, send_sem=s_sem, recv_sem=r_sem, device_id=device, device_id_type=MESH
        )

    load = pltpu.make_async_copy(x_ref, rows.at[0], load_sem)
    load.start()
    barrier = pltpu.get_barrier_semaphore()
    for dz in range(1, NZ):
        pl.semaphore_signal(barrier, inc=1, device_id=at(dz=dz), device_id_type=MESH)
    for dy in range(1, NY):
        pl.semaphore_signal(barrier, inc=1, device_id=at(dy=dy), device_id_type=MESH)
    for b in range(1, 8):
        pl.semaphore_signal(barrier, inc=1, device_id=at(dc=b % 2, dxl=b // 2 % 2, dxh=b // 4), device_id_type=MESH)
    load.wait()
    x = rows[0]
    mean = jnp.sum(x, axis=0, keepdims=True) * (1.0 / x.shape[0])
    coef = coef_ref[...]
    weighted = lax.dot_general(
        jnp.broadcast_to(coef, (8, coef.shape[1])), x - mean, (((1,), (0,)), ((), ())),
        precision=lax.Precision.HIGHEST, preferred_element_type=jnp.float32,
    )
    weight = jnp.broadcast_to(jnp.sum(coef, axis=1, keepdims=True), mean.shape)
    near[0, 0:1, :] = mean
    near[0, 1:2, :] = weighted[0:1, :]
    near[0, 2:3, :] = weight
    near[0, 3:4, :] = weight
    pl.semaphore_wait(barrier, NZ + NY + 8 - 3)

    near_copies = [
        remote(near.at[0], near.at[b], near_send.at[b - 1], near_recv.at[b - 1], at(dc=b % 2, dxl=b // 2))
        for b in range(1, 4)
    ]
    ring_copies = [
        remote(ring.at[0], ring.at[NZ - dz], ring_send.at[dz - 1], ring_recv.at[NZ - dz - 1], at(dz=dz))
        for dz in range(1, NZ)
    ]
    mean_copies = [
        remote(means.at[0], means.at[slot], mean_send.at[slot - 1], mean_recv.at[slot - 1], at(dy=dy))
        for slot, dy in ((2, 1), (1, -1), (3, 2))
    ]

    def to_up(g):
        return remote(rows.at[8 * g], rows.at[8 * g + 2], row_send.at[4 * g], row_recv.at[4 * g + 2], at(dy=1))

    def to_down(g):
        return remote(rows.at[8 * g], rows.at[8 * g + 1], row_send.at[4 * g + 1], row_recv.at[4 * g + 1], at(dy=-1))

    def half_down(g):
        top = pl.ds(0, 128)
        return remote(rows.at[8 * g + 1, top], rows.at[8 * g + 3, top], half_send.at[2 * g], half_recv.at[2 * g], at(dy=-1))

    def half_up(g):
        low = pl.ds(128, 128)
        return remote(rows.at[8 * g + 2, low], rows.at[8 * g + 3, low], half_send.at[2 * g + 1], half_recv.at[2 * g + 1], at(dy=1))

    def across():
        return remote(rows.at[0], rows.at[8], row_send.at[2], row_recv.at[0], at(dxl=1))

    def share(g, j):
        slot = 4 * g + j
        return remote(rows.at[8 * g + j], rows.at[8 * g + 4 + j], share_send.at[slot], row_recv.at[8 + slot], at(dc=1))

    for copy in near_copies:
        copy.start()
    across().start()
    to_up(0).start()
    to_down(0).start()
    share(0, 0).start()
    for copy in near_copies:
        copy.wait_recv()
    merged = merge(near[...])
    for row, value in enumerate(merged + (merged[2],)):
        ring[0, row : row + 1, :] = value
    for copy in ring_copies:
        copy.start()

    places = (h, lax.rem(9 - h, NZ))

    def piece(direction, idx):
        i, r = idx // CHUNKS, lax.rem(idx, CHUNKS)
        chunk_rows = pl.ds(pl.multiple_of(128 * direction + CHUNK_ROWS * lax.rem(r, 2), CHUNK_ROWS), CHUNK_ROWS)
        lanes = pl.ds(pl.multiple_of(LANES * (r // 2), LANES), LANES)
        return i, chunk_rows, lanes

    def chunk_copy(direction, idx, own):
        i, chunk_rows, lanes = piece(direction, idx)
        src = rows.at[i // 2] if own else cols.at[i]
        return remote(
            src.at[chunk_rows, lanes], cols.at[i, chunk_rows, lanes],
            send.at[direction, idx], recv.at[direction, idx], at(dz=1 - 2 * direction),
        )

    def extra_copy(direction, j, q):
        i = 2 * j + (1 - direction)
        half, lanes = pl.ds(128 * direction, 128), pl.ds(pl.multiple_of(256 * q, 256), 256)
        return remote(
            rows.at[j, half, lanes], cols.at[i, half, lanes],
            extra_send.at[direction, 4 * j + q], extra_recv.at[direction, 4 * j + q], at(dz=2 * direction - 1),
        )

    def source_of(direction, idx):
        e = lax.rem(idx // CHUNKS, 2)
        return e if direction == 0 else 1 - e

    def stream(n):
        for direction in range(2):
            place = places[direction]
            idx = n - place * LAG

            @pl.when(jnp.logical_and(idx >= 0, idx < STEPS))
            def _():
                source = source_of(direction, idx)

                @pl.when(place == source)
                def _():
                    chunk_copy(direction, idx, True).start()

                    @pl.when(jnp.logical_and(place == 1, lax.rem(idx, 4) == 3))
                    def _():
                        extra_copy(direction, idx // (2 * CHUNKS), lax.rem(idx, CHUNKS) // 4).start()

                @pl.when(jnp.logical_and(place != source, place >= 1))
                def _():
                    copy = chunk_copy(direction, idx, False)
                    copy.wait_recv()

                    @pl.when(place <= 6)
                    def _():
                        copy.start()

    def serve(n):
        @pl.when(n == 12)
        def _():
            for copy in ring_copies:
                copy.wait_recv()
            mean, update, weight = merge(ring[...])
            for row, value in enumerate((mean, update, weight, weight)):
                means[0, row : row + 1, :] = value
            update_ref[...] = update * (1.0 / 8192.0**0.5)
            for copy in mean_copies:
                copy.start()

        @pl.when(n == 2 * CHUNKS)
        def _():
            to_down(0).wait_recv()
            to_up(0).wait_recv()
            half_down(0).start()
            half_up(0).start()
            share(0, 1).start()
            share(0, 2).start()
            across().wait_recv()
            to_up(1).start()
            to_down(1).start()
            share(1, 0).start()

        @pl.when(n == 2 * CHUNKS + 8)
        def _():
            for copy in mean_copies:
                copy.wait_recv()

        @pl.when(n == 4 * CHUNKS)
        def _():
            half_down(0).wait_recv()
            half_up(0).wait_recv()
            share(0, 3).start()

        @pl.when(n == COMPUTE_AT + 2 * CHUNKS - 4)
        def _():
            to_down(1).wait_recv()
            to_up(1).wait_recv()
            half_down(1).start()
            half_up(1).start()
            share(1, 1).start()
            share(1, 2).start()

        @pl.when(n == COMPUTE_AT + 4 * CHUNKS - 12)
        def _():
            half_down(1).wait_recv()
            half_up(1).wait_recv()
            share(1, 3).start()

    def compute(n):
        t = n - COMPUTE_AT
        i, r = t // CHUNKS, lax.rem(t, CHUNKS)
        e, j = lax.rem(i, 2), i // 2

        @pl.when(jnp.logical_and(t >= 0, r == 0))
        def _():
            @pl.when(e == 0)
            def _():
                share(0, j).wait_recv()
                share(1, j).wait_recv()

            for direction in range(2):
                @pl.when(jnp.logical_and(places[direction] == 0, e == 1 - direction))
                def _():
                    for q in range(4):
                        extra_copy(direction, j, q).wait_recv()

            def convert(block):
                high, low = split(block - means[j, 0:1, :])
                col_hi[...] = high
                col_lo[...] = low

            @pl.when(h == e)
            def _():
                convert(rows[j])

            @pl.when(h != e)
            def _():
                convert(cols[i])

        @pl.when(jnp.logical_and(t >= 0, lax.rem(r, 2) == 0))
        def _():
            k = r // 2
            inner = pl.ds(pl.multiple_of(128 * lax.rem(k, 2), 128), 128)
            high, low = split(rows[4 * (k // 2) + j, inner, :] - means[j, 0:1, :])
            row_hi[...] = high
            row_lo[...] = low
            total = product(row_hi[...], col_hi[...])
            total += product(row_hi[...], col_lo[...])
            total += product(row_lo[...], col_hi[...])
            out = pl.ds(pl.multiple_of(128 * k, 128), 128)

            @pl.when(j == 0)
            def _():
                part[e, out, :] = total

            @pl.when(j != 0)
            def _():
                part[e, out, :] += total

    def part_copy(e, g, c):
        k = 2 * g + c
        slot = 4 * e + 2 * xh + core
        device = {"smp": (lax.rem(xl + g, 2) * NZ + z) * 2 + lax.rem(core + c, 2), "par": xl * NY + y}
        return remote(part.at[e, pl.ds(256 * k, 256)], landed.at[slot], part_send.at[4 * e + k], part_recv.at[slot], device)

    def hand_out(e):
        for g, c in ((1, 0), (1, 1), (0, 1)):
            part_copy(e, g, c).start()

        @pl.when(xl == xh)
        def _():
            landed[4 * e + 2 * xh + core] = part[e, 0:256, :]

        @pl.when(xl != xh)
        def _():
            part_copy(e, 0, 0).start()

    @pl.loop(0, STEPS + LATE)
    def _(n):
        serve(n)
        stream(n)
        compute(n)

    @pl.loop(STEPS + LATE, COMPUTE_END - CHUNKS)
    def _(n):
        compute(n)

    hand_out(0)

    @pl.loop(COMPUTE_END - CHUNKS, COMPUTE_END)
    def _(n):
        compute(n)

    hand_out(1)

    for copy in near_copies + ring_copies + mean_copies:
        copy.wait_send()
    for copy in (across(), to_up(0), to_down(0), to_up(1), to_down(1), half_down(0), half_up(0), half_down(1), half_up(1)):
        copy.wait_send()
    for g in range(2):
        for j in range(4):
            share(g, j).wait_send()

    @pl.loop(0, STEPS)
    def _(idx):
        for direction in range(2):
            place = places[direction]
            source = source_of(direction, idx)

            @pl.when(jnp.logical_or(place == source, jnp.logical_and(place >= 1, place <= 6)))
            def _():
                chunk_copy(direction, idx, False).wait_send()

    for direction in range(2):
        @pl.when(places[direction] == 1)
        def _():
            @pl.loop(0, 16)
            def _(q):
                extra_copy(direction, q // 4, lax.rem(q, 4)).wait_send()

    for e in range(2):
        for source_xh in range(2):
            for source_core in range(2):
                slot = 4 * e + 2 * source_xh + source_core
                own = jnp.logical_and(jnp.logical_and(xl == xh, xh == source_xh), core == source_core)

                @pl.when(jnp.logical_not(own))
                def _():
                    remote(part.at[0, pl.ds(0, 256)], landed.at[slot], part_send.at[0], part_recv.at[slot], at(dc=1)).wait_recv()

        for source_core in range(2):
            gram_ref[:, 256 * (2 * e + source_core) : 256 * (2 * e + source_core + 1)] = (
                landed[4 * e + source_core] + landed[4 * e + 2 + source_core]
            ) * (1.0 / 8192.0)

    for e in range(2):
        for g, c in ((1, 0), (1, 1), (0, 1)):
            part_copy(e, g, c).wait_send()

        @pl.when(xl != xh)
        def _():
            part_copy(e, 0, 0).wait_send()


def local(log_derivs, coefficients):
    count, width = log_derivs.shape
    dma = pltpu.SemaphoreType.DMA
    f32, bf16 = jnp.float32, jnp.bfloat16
    gram, update = pl.pallas_call(
        kernel,
        out_shape=(jax.ShapeDtypeStruct((count, width), f32), jax.ShapeDtypeStruct((1, width), f32)),
        in_specs=[pl.BlockSpec(memory_space=pl.ANY), pl.BlockSpec(memory_space=pltpu.VMEM)],
        out_specs=(pl.BlockSpec(memory_space=pltpu.VMEM), pl.BlockSpec(memory_space=pltpu.VMEM)),
        scratch_shapes=[
            pltpu.VMEM((16, count, width), f32),
            pltpu.VMEM((BLOCKS, count, width), f32),
            pltpu.VMEM((2, 4 * count, count), f32),
            pltpu.VMEM((8, count, count), f32),
            pltpu.VMEM((128, width), bf16),
            pltpu.VMEM((128, width), bf16),
            pltpu.VMEM((count, width), bf16),
            pltpu.VMEM((count, width), bf16),
            pltpu.VMEM((4, 4, width), f32),
            pltpu.VMEM((NZ, 4, width), f32),
            pltpu.VMEM((NY, 4, width), f32),
            dma(()), dma((3,)), dma((3,)), dma((NZ - 1,)), dma((NZ - 1,)), dma((3,)), dma((3,)),
            dma((8,)), dma((16,)), dma((4,)), dma((4,)), dma((8,)),
            dma((2, STEPS)), dma((2, STEPS)), dma((2, 16)), dma((2, 16)), dma((8,)), dma((8,)),
        ],
        compiler_params=pltpu.CompilerParams(collective_id=0, has_side_effects=True, vmem_limit_bytes=60 * 2**20),
    )(log_derivs, coefficients.reshape(1, count))
    start = lax.axis_index("smp") * (width // lax.axis_size("smp"))
    return gram, lax.dynamic_slice(update.reshape(width), (start,), (width // lax.axis_size("smp"),))


def solution(mesh):
    placed = (P("smp", "par"), P("smp"))
    return jax.shard_map(
        local,
        mesh=mesh,
        in_specs=placed,
        out_specs=(P("smp", "par"), P(("par", "smp"))),
        check_vma=False,
    )
```

time: 411 us -> 209 us (0.51)
  waiting for transfers between devices: 239 us -> 0 us
  Pallas kernels: 0 us -> 205 us
  blocking collectives: 117 us -> 0 us
  matrix products: 33.9 us -> 0 us
  between operations: 14.7 us -> 0.64 us
    pallas_call x0 -> x1, Pallas kernels: none -> 205 us  [local(): pl.pallas_call(kernel, out_shape=(jax.ShapeDtypeStruct((count, width), f3...]
    all_gather x1 -> x0, waiting for transfers between devices: 180 us -> none  [local(): lax.all_gather(centred, 'smp', axis=0, tiled=True)]
    psum x1 -> x0, blocking collectives: 59.2 us -> none  [local(): column_total = lax.psum(jnp.sum(log_derivs, axis=0), 'smp')]
    reduce_scatter x1 -> x0, waiting for transfers between devices: 58.5 us -> none  [local(): lax.psum_scatter(partial_gram, 'par', scatter_dimension=1, tiled=True)]
    unnamed x1 -> x0, blocking collectives: 57.8 us -> none
    dot_general x2 -> x0, matrix products: 33.9 us -> none  [the longest x1 33.2 us: row_products(): lax.dot_general(left_rows, right_rows, (((1,), (1,)), ((), ())), precisio...]
  transfers between devices with their start and end apart: 2 -> 0, of which waited for: 2 -> 0; matrix products, arithmetic and copies ran while one was open for 0% -> 0% of each run, Pallas kernels for 0% -> 0%
where the time goes in v1:
time: 209 us
  Pallas kernels  205 us (98%)
  local copies, waits for them, and re-layouts  3.5 us (2%)
    pallas_call x1, Pallas kernels, local(): pl.pallas_call(kernel, out_shape=(jax.ShapeDtypeStruct((count, width), f3...  205 us

profile of v1, /device:TPU:8, one launch (start us, length us, event | category | flops | bytes accessed | tf_op | source)
XLA Modules:
  0.0 208.9 jit_solution(1555621734981404111)
XLA Ops:
  0.6 204.8 %shard_map.41 = (f32[256,1024]{1,0:T(8,128)}, f32[1,1024]{1,0:T(1,128)}) custom-call(f32[256,1024]{1,0:T(8,128)} %x_ref.1, f32[1,256]{1,0:T(1,128)} %bitcast.3), custom_call_target="tpu_custom_call" | custom-call | tf_op jit(solution)/shard_map/pallas_call | solution.py:380
  205.4 1.2 dynamic-slice_bitcast_fusion
  206.6 2.3 %copy.5 = f32[256,1024]{1,0:T(8,128)} copy(f32[256,1024]{1,0:T(8,128)} %get-tuple-element.8) | data formatting | bytes 2097152

commit v2 on v0

v2 whole, which is shorter than its diff:
```python
import functools

import jax
import jax.numpy as jnp
from jax import lax
from jax.experimental import pallas as pl
from jax.experimental.pallas import tpu as pltpu
from jax.sharding import PartitionSpec as P

MESH = pl.DeviceIdType.MESH
NZ, NY = 8, 4
UNITS = 16
CHUNK_ROWS = 16
CHUNKS = 128 // CHUNK_ROWS
STEPS = UNITS * CHUNKS
HOP = 5
COMPUTE_AT = 38
EARLY = 8


def merge(stats):
    count = stats.shape[0]
    mean = jnp.sum(stats[:, 0:1, :], axis=0) * (1.0 / count)
    shift = stats[:, 0:1, :] - mean[None]
    update = jnp.sum(stats[:, 1:2, :] + stats[:, 2:3, :] * shift, axis=0)
    weight = jnp.sum(stats[:, 2:3, :], axis=0)
    return mean, update, weight


def split(values):
    high = values.astype(jnp.bfloat16)
    low = (values - high.astype(jnp.float32)).astype(jnp.bfloat16)
    return high, low


def product(left, right):
    return lax.dot_general(left, right, (((1,), (1,)), ((), ())), preferred_element_type=jnp.float32)


def kernel(
    x_ref, coef_ref, gram_ref, update_ref,
    rows, cols, part, landed, row_hi, row_lo, col_hi, col_lo, near, ring, means,
    load_sem, near_send, near_recv, ring_send, ring_recv, mean_send, mean_recv,
    row_send, row_recv, half_send, half_recv, share_send, send, recv, part_send, part_recv,
):
    smp, par = lax.axis_index("smp"), lax.axis_index("par")
    core, z, xl = lax.rem(smp, 2), lax.rem(smp // 2, NZ), smp // (2 * NZ)
    y, xh = lax.rem(par, NY), par // NY
    place = lax.rem((1 - 2 * core) * (z - 2 * y - 1) + 3 * NZ - core, NZ)
    onward = 1 - 2 * core
    relay = (place + 7) // 8
    behind = HOP * (place - 6 * (place // 7))

    def at(dz=0, dy=0, dc=0, dxl=0, dxh=0):
        zz, yy = lax.rem(z + dz + NZ, NZ), lax.rem(y + dy + NY, NY)
        cc, ll, hh = lax.rem(core + dc, 2), lax.rem(xl + dxl, 2), lax.rem(xh + dxh, 2)
        return {"smp": (ll * NZ + zz) * 2 + cc, "par": hh * NY + yy}

    def remote(src, dst, s_sem, r_sem, device):
        return pltpu.make_async_remote_copy(
            src_ref=src, dst_ref=dst, send_sem=s_sem, recv_sem=r_sem, device_id=device, device_id_type=MESH
        )

    load = pltpu.make_async_copy(x_ref, rows.at[0], load_sem)
    load.start()
    barrier = pltpu.get_barrier_semaphore()
    for dz in range(1, NZ):
        pl.semaphore_signal(barrier, inc=1, device_id=at(dz=dz), device_id_type=MESH)
    for dy in range(1, NY):
        pl.semaphore_signal(barrier, inc=1, device_id=at(dy=dy), device_id_type=MESH)
    for b in range(1, 8):
        pl.semaphore_signal(barrier, inc=1, device_id=at(dc=b % 2, dxl=b // 2 % 2, dxh=b // 4), device_id_type=MESH)
    load.wait()
    pl.semaphore_wait(barrier, NZ + NY + 8 - 3)

    near_copies = [
        remote(near.at[0], near.at[b], near_send.at[b - 1], near_recv.at[b - 1], at(dc=b % 2, dxl=b // 2))
        for b in range(1, 4)
    ]
    ring_copies = [
        remote(ring.at[0], ring.at[NZ - dz], ring_send.at[dz - 1], ring_recv.at[NZ - dz - 1], at(dz=dz))
        for dz in range(1, NZ)
    ]
    mean_copies = [
        remote(means.at[0], means.at[slot], mean_send.at[slot - 1], mean_recv.at[slot - 1], at(dy=dy))
        for slot, dy in ((2, 1), (1, -1), (3, 2))
    ]

    def to_up(g):
        return remote(rows.at[8 * g], rows.at[8 * g + 2], row_send.at[4 * g], row_recv.at[4 * g + 2], at(dy=1))

    def to_down(g):
        return remote(rows.at[8 * g], rows.at[8 * g + 1], row_send.at[4 * g + 1], row_recv.at[4 * g + 1], at(dy=-1))

    def half_down(g):
        top = pl.ds(0, 128)
        return remote(rows.at[8 * g + 1, top], rows.at[8 * g + 3, top], half_send.at[2 * g], half_recv.at[2 * g], at(dy=-1))

    def half_up(g):
        low = pl.ds(128, 128)
        return remote(rows.at[8 * g + 2, low], rows.at[8 * g + 3, low], half_send.at[2 * g + 1], half_recv.at[2 * g + 1], at(dy=1))

    def across():
        return remote(rows.at[0], rows.at[8], row_send.at[2], row_recv.at[0], at(dxl=1))

    def share(g, j):
        slot = 4 * g + j
        return remote(rows.at[8 * g + j], rows.at[8 * g + 4 + j], share_send.at[slot], row_recv.at[8 + slot], at(dc=1))

    def unit(u):
        q, v = u // 4, lax.rem(u, 4)
        third, fourth = (q // 2) * (1 - lax.rem(q, 2)), (q // 2) * lax.rem(q, 2)
        first = 1 - q // 2
        j = first * q + third * (2 + v // 2) + fourth * (2 + lax.rem(v, 2))
        f = first * v + third * lax.rem(v, 2) + fourth * (2 + v // 2)
        return j, f

    def home(j, f):
        return 4 * (f // 2) + j, 128 * lax.rem(f, 2)

    def chunk_copy(idx, own, way):
        j, f = unit(idx // CHUNKS)
        r = CHUNK_ROWS * lax.rem(idx, CHUNKS)
        target = cols.at[j, pl.ds(pl.multiple_of(128 * f + r, CHUNK_ROWS), CHUNK_ROWS)]
        if own:
            block, offset = home(j, f)
            source = rows.at[block, pl.ds(pl.multiple_of(offset + r, CHUNK_ROWS), CHUNK_ROWS)]
        else:
            source = target
        dz = onward if way == 0 else -onward
        return remote(source, target, send.at[way, idx], recv.at[idx], at(dz=dz))

    def stream(idx):
        @pl.when(place == 0)
        def _():
            chunk_copy(idx, True, 0).start()
            chunk_copy(idx, True, 1).start()

        @pl.when(place >= 1)
        def _():
            copy = chunk_copy(idx, False, 0)
            copy.wait_recv()

            @pl.when(place <= 5)
            def _():
                copy.start()

    def serve(idx):
        n = idx + behind

        @pl.when(idx == 8 * (1 - relay))
        def _():
            for copy in ring_copies:
                copy.wait_recv()
            mean, update, weight = merge(ring[...])
            for row, value in enumerate((mean, update, weight, weight)):
                means[0, row : row + 1, :] = value
            update_ref[...] = update * (1.0 / 8192.0**0.5)
            for copy in mean_copies:
                copy.start()

        @pl.when(n == 32)
        def _():
            to_down(0).wait_recv()
            to_up(0).wait_recv()
            share(0, 1).start()
            share(0, 2).start()
            across().wait_recv()
            to_up(1).start()
            to_down(1).start()
            share(1, 0).start()
            half_down(0).start()
            half_up(0).start()

        @pl.when(n == 32 + 5 * relay)
        def _():
            share(0, 1).wait_recv()
            share(0, 2).wait_recv()
            share(1, 0).wait_recv()
            for copy in mean_copies:
                copy.wait_recv()

        @pl.when(n == 66)
        def _():
            to_down(1).wait_recv()
            to_up(1).wait_recv()
            share(1, 1).start()
            share(1, 2).start()
            half_down(1).start()
            half_up(1).start()

        @pl.when(n == 72)
        def _():
            share(1, 1).wait_recv()
            share(1, 2).wait_recv()

        @pl.when(n == 80)
        def _():
            half_down(0).wait_recv()
            half_up(0).wait_recv()
            share(0, 3).start()

        @pl.when(n == 80 + 5 * relay)
        def _():
            share(0, 3).wait_recv()

        @pl.when(n == 108)
        def _():
            half_down(1).wait_recv()
            half_up(1).wait_recv()
            share(1, 3).start()

        @pl.when(n == 116)
        def _():
            share(1, 3).wait_recv()

    def part_copy(f, k):
        slot = 4 * f + 2 * xh + core
        device = {"smp": (lax.rem(xl + k // 2, 2) * NZ + z) * 2 + lax.rem(core + k, 2), "par": xl * NY + y}
        block = pl.ds(pl.multiple_of(256 * k, 256), 256)
        return remote(part.at[f, block], landed.at[slot], part_send.at[4 * f + k], part_recv.at[slot], device)

    def stays(k):
        return jnp.logical_and(xl == xh, k == 0)

    def compute(idx):
        t = idx + behind - COMPUTE_AT
        u, k = t // CHUNKS, lax.rem(t, CHUNKS)
        j, f = unit(u)
        tile = pl.ds(pl.multiple_of(128 * k, 128), 128)

        @pl.when(jnp.logical_and(t >= 0, t < STEPS))
        def _():
            @pl.when(k == 0)
            def _():
                def convert(block):
                    high, low = split(block - means[j, 0:1, :])
                    col_hi[...] = high
                    col_lo[...] = low

                @pl.when(place == 0)
                def _():
                    block, offset = home(j, f)
                    convert(rows[block, pl.ds(pl.multiple_of(offset, 128), 128), :])

                @pl.when(place != 0)
                def _():
                    convert(cols[j, pl.ds(pl.multiple_of(128 * f, 128), 128), :])

            @pl.when(f == 0)
            def _():
                inner = pl.ds(pl.multiple_of(128 * lax.rem(k, 2), 128), 128)
                high, low = split(rows[4 * (k // 2) + j, inner, :] - means[j, 0:1, :])
                row_hi[j, tile, :] = high
                row_lo[j, tile, :] = low

            total = product(row_hi[j, tile, :], col_hi[...])
            total += product(row_hi[j, tile, :], col_lo[...])
            total += product(row_lo[j, tile, :], col_hi[...])

            @pl.when(j == 0)
            def _():
                part[f, tile, :] = total

            @pl.when(j != 0)
            def _():
                part[f, tile, :] += total

            @pl.when(jnp.logical_and(j == 3, lax.rem(k, 2) == 1))
            def _():
                @pl.when(stays(k // 2))
                def _():
                    landed[4 * f + 2 * xh + core] = part[f, 0:256, :]

                @pl.when(jnp.logical_not(stays(k // 2)))
                def _():
                    part_copy(f, k // 2).start()

    @pl.when(place == 0)
    def _():
        @pl.loop(0, EARLY)
        def _(idx):
            stream(idx)

    to_up(0).start()
    to_down(0).start()
    x = rows[0]
    mean = jnp.sum(x, axis=0, keepdims=True) * (1.0 / x.shape[0])
    coef = coef_ref[...]
    weighted = lax.dot_general(
        jnp.broadcast_to(coef, (8, coef.shape[1])), x - mean, (((1,), (0,)), ((), ())),
        precision=lax.Precision.HIGHEST, preferred_element_type=jnp.float32,
    )
    weight = jnp.broadcast_to(jnp.sum(coef, axis=1, keepdims=True), mean.shape)
    near[0, 0:1, :] = mean
    near[0, 1:2, :] = weighted[0:1, :]
    near[0, 2:3, :] = weight
    near[0, 3:4, :] = weight
    for copy in near_copies:
        copy.start()
    across().start()
    share(0, 0).start()
    for copy in near_copies:
        copy.wait_recv()
    merged = merge(near[...])
    for row, value in enumerate(merged + (merged[2],)):
        ring[0, row : row + 1, :] = value
    for copy in ring_copies:
        copy.start()
    share(0, 0).wait_recv()

    @pl.loop(0, STEPS)
    def _(idx):
        serve(idx)

        @pl.when(idx >= EARLY * (1 - relay))
        def _():
            stream(idx)

        compute(idx)

    @pl.loop(STEPS, STEPS + COMPUTE_AT)
    def _(idx):
        serve(idx)
        compute(idx)

    for f in range(4):
        for source_xh in range(2):
            for source_core in range(2):
                slot = 4 * f + 2 * source_xh + source_core
                own = jnp.logical_and(jnp.logical_and(xl == xh, xh == source_xh), core == source_core)

                @pl.when(jnp.logical_not(own))
                def _():
                    remote(part.at[0, pl.ds(0, 256)], landed.at[slot], part_send.at[0], part_recv.at[slot], at(dc=1)).wait_recv()

        for source_core in range(2):
            first = 512 * (1 - source_core) + 256 * ((source_core + f // 2) % 2) + 128 * (f % 2)
            gram_ref[:, first : first + 128] = (landed[4 * f + source_core] + landed[4 * f + 2 + source_core]) * (1.0 / 8192.0)

    for copy in near_copies + ring_copies + mean_copies:
        copy.wait_send()
    for copy in (across(), to_up(0), to_down(0), to_up(1), to_down(1), half_down(0), half_up(0), half_down(1), half_up(1)):
        copy.wait_send()
    for g in range(2):
        for j in range(4):
            share(g, j).wait_send()

    @pl.loop(0, STEPS)
    def _(idx):
        @pl.when(place <= 5)
        def _():
            chunk_copy(idx, False, 0).wait_send()

        @pl.when(place == 0)
        def _():
            chunk_copy(idx, True, 1).wait_send()

    @pl.loop(0, 4)
    def _(f):
        for k in range(4):
            @pl.when(jnp.logical_not(stays(k)))
            def _():
                part_copy(f, k).wait_send()


def local(log_derivs, coefficients):
    count, width = log_derivs.shape
    dma = pltpu.SemaphoreType.DMA
    f32, bf16 = jnp.float32, jnp.bfloat16
    gram, update = pl.pallas_call(
        kernel,
        out_shape=(jax.ShapeDtypeStruct((count, width), f32), jax.ShapeDtypeStruct((1, width), f32)),
        in_specs=[pl.BlockSpec(memory_space=pl.ANY), pl.BlockSpec(memory_space=pltpu.VMEM)],
        out_specs=(pl.BlockSpec(memory_space=pltpu.VMEM), pl.BlockSpec(memory_space=pltpu.VMEM)),
        scratch_shapes=[
            pltpu.VMEM((16, count, width), f32),
            pltpu.VMEM((NY, 2 * count, width), f32),
            pltpu.VMEM((4, 4 * count, count // 2), f32),
            pltpu.VMEM((16, count, count // 2), f32),
            pltpu.VMEM((NY, 4 * count, width), bf16),
            pltpu.VMEM((NY, 4 * count, width), bf16),
            pltpu.VMEM((count // 2, width), bf16),
            pltpu.VMEM((count // 2, width), bf16),
            pltpu.VMEM((4, 4, width), f32),
            pltpu.VMEM((NZ, 4, width), f32),
            pltpu.VMEM((NY, 4, width), f32),
            dma(()), dma((3,)), dma((3,)), dma((NZ - 1,)), dma((NZ - 1,)), dma((3,)), dma((3,)),
            dma((8,)), dma((16,)), dma((4,)), dma((4,)), dma((8,)),
            dma((2, STEPS)), dma((STEPS,)), dma((16,)), dma((16,)),
        ],
        compiler_params=pltpu.CompilerParams(collective_id=0, has_side_effects=True, vmem_limit_bytes=60 * 2**20),
    )(log_derivs, coefficients.reshape(1, count))
    start = lax.axis_index("smp") * (width // lax.axis_size("smp"))
    return gram, lax.dynamic_slice(update.reshape(width), (start,), (width // lax.axis_size("smp"),))


def solution(mesh):
    placed = (P("smp", "par"), P("smp"))
    return jax.shard_map(
        local,
        mesh=mesh,
        in_specs=placed,
        out_specs=(P("smp", "par"), P(("par", "smp"))),
        check_vma=False,
    )
```

time: 411 us -> 150 us (0.36)
  waiting for transfers between devices: 239 us -> 0 us
  Pallas kernels: 0 us -> 144 us
  blocking collectives: 117 us -> 0 us
  matrix products: 33.9 us -> 0 us
  between operations: 14.7 us -> 0.64 us
    all_gather x1 -> x0, waiting for transfers between devices: 180 us -> none  [local(): lax.all_gather(centred, 'smp', axis=0, tiled=True)]
    pallas_call x0 -> x1, Pallas kernels: none -> 144 us  [local(): pl.pallas_call(kernel, out_shape=(jax.ShapeDtypeStruct((count, width), f3...]
    psum x1 -> x0, blocking collectives: 59.2 us -> none  [local(): column_total = lax.psum(jnp.sum(log_derivs, axis=0), 'smp')]
    reduce_scatter x1 -> x0, waiting for transfers between devices: 58.5 us -> none  [local(): lax.psum_scatter(partial_gram, 'par', scatter_dimension=1, tiled=True)]
    unnamed x1 -> x0, blocking collectives: 57.8 us -> none
    dot_general x2 -> x0, matrix products: 33.9 us -> none  [the longest x1 33.2 us: row_products(): lax.dot_general(left_rows, right_rows, (((1,), (1,)), ((), ())), precisio...]
  transfers between devices with their start and end apart: 2 -> 0, of which waited for: 2 -> 0; matrix products, arithmetic and copies ran while one was open for 0% -> 0% of each run, Pallas kernels for 0% -> 0%
where the time goes in v2:
time: 150 us; the launch traced here: 148 us
  Pallas kernels  144 us (96%)
  local copies, waits for them, and re-layouts  3.5 us (2%)
    pallas_call x1, Pallas kernels, local(): pl.pallas_call(kernel, out_shape=(jax.ShapeDtypeStruct((count, width), f3...  144 us

profile of v2, /device:TPU:8, one launch (start us, length us, event | category | flops | bytes accessed | tf_op | source)
XLA Modules:
  0.0 148.0 jit_solution(17126811731074700366)
XLA Ops:
  0.6 143.8 %shard_map.41 = (f32[256,1024]{1,0:T(8,128)}, f32[1,1024]{1,0:T(1,128)}) custom-call(f32[256,1024]{1,0:T(8,128)} %x_ref.1, f32[1,256]{1,0:T(1,128)} %bitcast.3), custom_call_target="tpu_custom_call" | custom-call | tf_op jit(solution)/shard_map/pallas_call | solution.py:371
  144.5 1.2 dynamic-slice_bitcast_fusion
  145.6 2.3 %copy.5 = f32[256,1024]{1,0:T(8,128)} copy(f32[256,1024]{1,0:T(8,128)} %get-tuple-element.8) | data formatting | bytes 2097152

commit v3 on v2

--- a/solution.py
+++ b/solution.py
@@ -128,7 +128,7 @@
         else:
             source = target
         dz = onward if way == 0 else -onward
-        return remote(source, target, send.at[way, idx], recv.at[idx], at(dz=dz))
+        return remote(source, target, send.at[way], recv.at[idx], at(dz=dz))
 
     def stream(idx):
         @pl.when(place == 0)
@@ -225,11 +225,12 @@
 
     def compute(idx):
         t = idx + behind - COMPUTE_AT
-        u, k = t // CHUNKS, lax.rem(t, CHUNKS)
+        u, r = t // CHUNKS, lax.rem(t, CHUNKS)
+        k = r // 2
         j, f = unit(u)
-        tile = pl.ds(pl.multiple_of(128 * k, 128), 128)
-
-        @pl.when(jnp.logical_and(t >= 0, t < STEPS))
+        tile = pl.ds(pl.multiple_of(256 * k, 256), 256)
+
+        @pl.when(jnp.logical_and(jnp.logical_and(t >= 0, t < STEPS), lax.rem(r, 2) == 0))
         def _():
             @pl.when(k == 0)
             def _():
@@ -249,8 +250,7 @@
 
             @pl.when(f == 0)
             def _():
-                inner = pl.ds(pl.multiple_of(128 * lax.rem(k, 2), 128), 128)
-                high, low = split(rows[4 * (k // 2) + j, inner, :] - means[j, 0:1, :])
+                high, low = split(rows[4 * k + j] - means[j, 0:1, :])
                 row_hi[j, tile, :] = high
                 row_lo[j, tile, :] = low
 
@@ -266,15 +266,15 @@
             def _():
                 part[f, tile, :] += total
 
-            @pl.when(jnp.logical_and(j == 3, lax.rem(k, 2) == 1))
-            def _():
-                @pl.when(stays(k // 2))
+            @pl.when(j == 3)
+            def _():
+                @pl.when(stays(k))
                 def _():
                     landed[4 * f + 2 * xh + core] = part[f, 0:256, :]
 
-                @pl.when(jnp.logical_not(stays(k // 2)))
+                @pl.when(jnp.logical_not(stays(k)))
                 def _():
-                    part_copy(f, k // 2).start()
+                    part_copy(f, k).start()
 
     @pl.when(place == 0)
     def _():
@@ -319,7 +319,7 @@
 
         compute(idx)
 
-    @pl.loop(STEPS, STEPS + COMPUTE_AT)
+    @pl.loop(STEPS, STEPS + COMPUTE_AT - behind)
     def _(idx):
         serve(idx)
         compute(idx)
@@ -346,15 +346,13 @@
         for j in range(4):
             share(g, j).wait_send()
 
-    @pl.loop(0, STEPS)
-    def _(idx):
-        @pl.when(place <= 5)
-        def _():
-            chunk_copy(idx, False, 0).wait_send()
-
-        @pl.when(place == 0)
-        def _():
-            chunk_copy(idx, True, 1).wait_send()
+    @pl.when(place <= 5)
+    def _():
+        remote(cols, cols, send.at[0], recv.at[0], at(dz=onward)).wait_send()
+
+    @pl.when(place == 0)
+    def _():
+        remote(cols, cols, send.at[1], recv.at[0], at(dz=onward)).wait_send()
 
     @pl.loop(0, 4)
     def _(f):
@@ -387,7 +385,7 @@
             pltpu.VMEM((NY, 4, width), f32),
             dma(()), dma((3,)), dma((3,)), dma((NZ - 1,)), dma((NZ - 1,)), dma((3,)), dma((3,)),
             dma((8,)), dma((16,)), dma((4,)), dma((4,)), dma((8,)),
-            dma((2, STEPS)), dma((STEPS,)), dma((16,)), dma((16,)),
+            dma((2,)), dma((STEPS,)), dma((16,)), dma((16,)),
         ],
         compiler_params=pltpu.CompilerParams(collective_id=0, has_side_effects=True, vmem_limit_bytes=60 * 2**20),
     )(log_derivs, coefficients.reshape(1, count))

time: 150 us -> 144 us (0.960)
  Pallas kernels: 144 us -> 138 us
    pallas_call x1, Pallas kernels: 144 us -> 138 us  [local(): pl.pallas_call(kernel, out_shape=(jax.ShapeDtypeStruct((count, width), f3...]
where the time goes in v3:
time: 144 us; the launch traced here: 142 us
  Pallas kernels  138 us (96%)
  local copies, waits for them, and re-layouts  3.5 us (2%)
    pallas_call x1, Pallas kernels, local(): pl.pallas_call(kernel, out_shape=(jax.ShapeDtypeStruct((count, width), f3...  138 us

profile of v3, /device:TPU:8, one launch (start us, length us, event | category | flops | bytes accessed | tf_op | source)
XLA Modules:
  0.0 142.2 jit_solution(11013798204048225466)
XLA Ops:
  0.6 138.1 %shard_map.41 = (f32[256,1024]{1,0:T(8,128)}, f32[1,1024]{1,0:T(1,128)}) custom-call(f32[256,1024]{1,0:T(8,128)} %x_ref.1, f32[1,256]{1,0:T(1,128)} %bitcast.3), custom_call_target="tpu_custom_call" | custom-call | tf_op jit(solution)/shard_map/pallas_call | solution.py:369
  138.7 1.2 dynamic-slice_bitcast_fusion
  139.9 2.3 %copy.5 = f32[256,1024]{1,0:T(8,128)} copy(f32[256,1024]{1,0:T(8,128)} %get-tuple-element.8) | data formatting | bytes 2097152
